TPU v7x, 256 devices: a whole 4x4x8 slice. The times are simulated.
256 devices in a mesh: lon: 32 (over y, z), lat: 8 (over x, core).
Axes of the slice: x: 4, y: 4, z: 8, core: 2. Of those that a mesh axis runs over, the one named last changes fastest.
Arguments:
- height: float32 [1024, 512, 1024], P(None, 'lon', 'lat'), may hold values from -1 to 1
- land_sea: int32 [512, 1024], P('lon', 'lat'), may hold values 0 or 1
- patterns: bfloat16 [512, 2, 512, 1024], P(None, None, 'lon', 'lat'), may hold values from -0.01171875 to 0.01171875
Outputs:
- covariance: float32 [32, 512, 512], P('lon', 'lat')
All inputs are finite; a program needn't handle non-finite values. No bound on the sum of `land_sea` on one device may be relied on, other than what follows from the above.
Results may differ from a plain program's by a relative error of at most 0.0003.
The roundings to bfloat16 on the way count: a program that leaves them out, or rounds other values in their place, can miss the bound.
Values sent between devices are 32-bit elements; how exact they have to be, the bound alone decides.
A program may use at most 128 MiB of HBM per device.

v0:
```python
import math
import jax
import jax.numpy as jnp
from jax import lax
from jax.sharding import PartitionSpec as P

LAG_DEV = 1
GRAVITY = 9.81
ROTATION = 7.2921e-05
EARTH_RADIUS = 6371000.0
LAT_SOUTH = 20.0
LAT_SPAN = 45.0
LON_STEP = 1.0 / 12.0


def padded_2(shard, sides, width):
    for axis, dim in sides:
        devices, length = (lax.axis_size(axis), shard.shape[dim])
        up = [(i, (i + 1) % devices) for i in range(devices - 1)]
        down = [(j, i) for i, j in up]
        last = lax.slice_in_dim(shard, length - width, length, axis=dim)
        initial = lax.slice_in_dim(shard, 0, width, axis=dim)
        before = lax.ppermute(last, axis, up)
        after = lax.ppermute(initial, axis, down)
        shard = jnp.concatenate([before, shard, after], axis=dim)
    return shard


def stencil_coefs(rows_index, total_rows):
    degrees = LAT_SOUTH + LAT_SPAN * (rows_index.astype(jnp.float32) + 0.5) / total_rows
    radians = degrees * (math.pi / 180.0)
    coriolis = 2.0 * ROTATION * jnp.sin(radians)
    north_step = EARTH_RADIUS * (LAT_SPAN / total_rows) * (math.pi / 180.0)
    east_step = EARTH_RADIUS * jnp.cos(radians) * (LON_STEP * math.pi / 180.0)
    return (-GRAVITY / (coriolis * 2.0 * north_step), GRAVITY / (coriolis * 2.0 * east_step))


def velocities(padded, coef_east, coef_north, ocean):
    lat_diff = padded[:, 1:-1, 2:] - padded[:, 1:-1, :-2]
    lon_diff = padded[:, 2:, 1:-1] - padded[:, :-2, 1:-1]
    return (coef_east * lat_diff * ocean, coef_north * lon_diff * ocean)


def on_device(height, land_sea, patterns):
    days, lon_cells, lat_cells = height.shape
    lat_devices = lax.axis_size("lat")
    lon_devices = lax.axis_size("lon")
    total_rows = lat_cells * lat_devices
    lat_place = lax.axis_index("lat")
    lon_place = lax.axis_index("lon")
    rows_index = lat_place * lat_cells + jnp.arange(lat_cells, dtype=jnp.int32)
    coef_east, coef_north = stencil_coefs(rows_index, total_rows)
    ocean = land_sea.astype(jnp.float32)
    padded = padded_2(height, (("lon", 1), ("lat", 2)), 1)
    east_vel, north_vel = velocities(padded, coef_east, coef_north, ocean)
    local_energy = jnp.sum(east_vel * east_vel + north_vel * north_vel)
    stacked = (
        jnp.stack([east_vel, north_vel], axis=1)
        .astype(jnp.bfloat16)
        .reshape(days, 2 * lon_cells * lat_cells)
    )
    mode_count = patterns.shape[0]
    owned = mode_count // lat_devices
    flat_patterns = patterns.reshape(mode_count, 2 * lon_cells * lat_cells)
    energy = lax.psum(local_energy, ("lon", "lat"))
    totals = lax.psum(
        lax.dot_general(
            flat_patterns, stacked, (((1,), (1,)), ((), ())), preferred_element_type=jnp.float32
        ),
        ("lon", "lat"),
    )
    cell_total = 2.0 * days * lon_cells * lon_devices * total_rows
    centered = totals - jnp.mean(totals, axis=1, keepdims=True)
    normed = centered / jnp.sqrt(energy / cell_total + 1e-06)
    my_rows = lax.dynamic_slice_in_dim(normed, lat_place * owned, owned, 0)
    padded_rows = jnp.concatenate([my_rows, jnp.zeros_like(my_rows)], axis=1)
    lag = lon_place * LAG_DEV + 0
    shifted = lax.dynamic_slice_in_dim(padded_rows, lag, days, 1)
    product = lax.dot_general(
        shifted,
        normed,
        (((1,), (1,)), ((), ())),
        precision=lax.Precision.HIGHEST,
        preferred_element_type=jnp.float32,
    )
    results = [product / (days - lag).astype(jnp.float32)]
    return jnp.stack(results, axis=0)


def solution(mesh):
    placed = (P(None, "lon", "lat"), P("lon", "lat"), P(None, None, "lon", "lat"))
    return jax.shard_map(
        on_device, mesh=mesh, in_specs=placed, out_specs=P("lon", "lat", None), check_vma=False
    )
```

profile of v0, /device:TPU:2, one launch (start us, length us, event | category | flops | bytes accessed | tf_op | source)
XLA Modules:
  0.0 381.3 jit_solution(7635947852473987990)
XLA Ops:
  6.5 0.0 copy-start.2
  6.5 0.0 all-reduce.3.cloned.1.call-start
  6.5 6.1 %copy.10 = f32[1024,16,128]{2,0,1:T(8,128)S(1)} copy(f32[1024,16,128]{2,1,0:T(8,128)} %param.3) | data formatting | bytes 16777216 | tf_op args[0]
  12.6 0.0 copy-start.1
  12.6 3.3 copy-done.1
  15.9 0.1 fusion.23
  16.0 3.9 %collective-permute-start = (f32[1024,1,128]{2,0,1:T(8,128)S(1)}, f32[1024,1,128]{2,0,1:T(8,128)S(1)}, u32[]{:S(2)}, u32[]{:S(2)}) collective-permute-start(f32[1024,1,128]{2,0,1:T(8,128)S(1)} %get-tuple-element.11), channel_id=1, source_target_pairs={{0,8},{8,16},{16,24},{24,32},{32,40},{40,48},{48,56},{56,64},{64,7... | collective-permute-start | bytes 1572872 | tf_op jit(solution)/shard_map/ppermute | solution.py:23
  19.9 1.3 collective-permute-start.1
  21.2 0.0 copy-done.2
  21.2 9.8 %collective-permute-done = f32[1024,1,128]{2,0,1:T(8,128)S(1)} collective-permute-done((f32[1024,1,128]{2,0,1:T(8,128)S(1)}, f32[1024,1,128]{2,0,1:T(8,128)S(1)}, u32[]{:S(2)}, u32[]{:S(2)}) %collective-permute-start) | collective-permute-done | bytes 524320 | tf_op jit(solution)/shard_map/ppermute | solution.py:23
  31.0 5.8 %constant_dynamic-update-slice_fusion.1 = f32[1024,18,128]{2,0,1:T(8,128)S(1)} fusion(f32[1024,18,128]{2,0,1:T(8,128)S(1)} %constant_dynamic-update-slice_fusion.2, f32[1024,16,128]{2,1,0:T(8,128)} %param.3), kind=kLoop, calls=%fused_computation.24 | loop fusion | bytes 16777216
  36.8 0.0 collective-permute-done.1
  36.9 0.0 copy-start
  36.9 8.4 %fusion.22 = (f32[1024,18,1]{2,0,1:T(8,128)}, f32[1024,18,1]{2,0,1:T(8,128)}) fusion(f32[1024,18,128]{2,0,1:T(8,128)S(1)} %constant_dynamic-update-slice_fusion), kind=kLoop, calls=%fused_computation.35 | loop fusion | bytes 294912 | tf_op jit(solution)/shard_map/slice | solution.py:22
  45.3 0.9 copy-done
  46.2 5.6 %copy.13 = f32[1024,18,1]{0,2,1:T(1,128)S(1)} copy(f32[1024,18,1]{2,0,1:T(8,128)} %get-tuple-element.8) | data formatting | bytes 147456 | tf_op jit(solution)/shard_map/slice | solution.py:22
  51.8 1.9 collective-permute-start.2
  53.7 5.6 %copy.15 = f32[1024,18,1]{0,2,1:T(1,128)S(1)} copy(f32[1024,18,1]{2,0,1:T(8,128)} %get-tuple-element.9) | data formatting | bytes 147456 | tf_op jit(solution)/shard_map/slice | solution.py:21
  59.3 2.6 collective-permute-start.3
  61.9 0.1 multiply_divide_fusion
  62.0 0.0 collective-permute-done.2
  62.0 5.1 %copy.14 = f32[1024,18,1]{2,0,1:T(8,128)} copy(f32[1024,18,1]{0,2,1:T(1,128)S(1)} %collective-permute-done.2) | data formatting | bytes 147456 | tf_op jit(solution)/shard_map/ppermute | solution.py:24
  67.1 0.0 collective-permute-done.3
  67.1 5.2 %copy.16 = f32[1024,18,1]{2,0,1:T(8,128)} copy(f32[1024,18,1]{0,2,1:T(1,128)S(1)} %collective-permute-done.3) | data formatting | bytes 147456 | tf_op jit(solution)/shard_map/ppermute | solution.py:23
  72.2 18.3 %add_reduce_fusion = (f32[]{:T(128)}, bf16[1024,16,128]{2,0,1:T(8,128)(2,1)S(1)}, bf16[1024,1,16,128]{3,0,2,1:T(8,128)(2,1)S(1)}) fusion(f32[16,128]{1,0:T(8,128)S(1)} %convert_element_type.18, f32[1024,16,128]{2,0,1:T(8,128)} %copy-done.1, f32[1024,1,128]{2,0,1:T(8,128)S(1)} %collective-permute-done, f32[1024,1,128]{2,0,1:T(8,128)S(1)} %collective-permute-done.1, ...), kind=kLoop, calls=%fused_computation.14 | loop fusion | flops 33554432 | bytes 27419652 | tf_op jit(solution)/shard_map/reduce_sum | solution.py:56
  90.5 8.1 %fusion.11 = f32[512,1024]{0,1:T(8,128)} fusion(bf16[512,2,16,128]{3,2,1,0:T(8,128)(2,1)} %param.5, bf16[1024,1,16,128]{3,0,2,1:T(8,128)(2,1)S(1)} %get-tuple-element.7, bf16[1024,1,16,128]{3,0,2,1:T(8,128)(2,1)S(1)} %bitcast.14), kind=kOutput, calls=%fused_computation.19 | convolution fusion | flops 4299161600 | bytes 14680064 | tf_op jit(solution)/shard_map/dot_general | solution.py:67
  98.6 0.0 all-reduce.3.cloned.1.call-update
  98.7 80.3 %psum.15 = f32[]{:T(128)} all-reduce(f32[]{:T(128)} %get-tuple-element.5), channel_id=1, replica_groups=mesh['lon'=32,'lat'=8] {'lon','lat'}, use_global_device_ids=true, to_apply=%region_3.0 | all-reduce | flops 1 | bytes 8 | tf_op jit(solution)/shard_map/psum | solution.py:65
  179.7 188.9 %all-reduce.3.cloned.1.call-done = f32[512,1024]{0,1:T(8,128)} async-done(((f32[512,1024]{0,1:T(8,128)}), f32[512,1024]{0,1:T(8,128)}) %all-reduce.3.cloned.1.call-update) | async-done | bytes 2097168 | tf_op jit(solution)/shard_map/psum | solution.py:66
  368.6 1.8 reduce_sum.18
  370.4 1.9 subtract_divide_fusion
  372.2 0.2 constant_dynamic-slice_fusion
  372.4 2.0 fusion.16
  (4 shorter events, 0.1 us)
Async XLA Ops:
  6.5 14.6 %copy-start.2 = (s32[16,128]{1,0:T(8,128)S(1)}, s32[16,128]{1,0:T(8,128)}, u32[]{:S(2)}) copy-start(s32[16,128]{1,0:T(8,128)} %param.4) | copy-start | bytes 24580
  6.5 362.0 %all-reduce.3.cloned.1.call-start = ((), (), s32[]{:S(2)}) async-start(), calls=%async_computation | async-start | bytes 4194304 | tf_op jit(solution)/shard_map/psum | solution.py:66
  12.6 3.3 copy-start.1
  16.0 15.0 %collective-permute-start = (f32[1024,1,128]{2,0,1:T(8,128)S(1)}, f32[1024,1,128]{2,0,1:T(8,128)S(1)}, u32[]{:S(2)}, u32[]{:S(2)}) collective-permute-start(f32[1024,1,128]{2,0,1:T(8,128)S(1)} %get-tuple-element.11), channel_id=1, source_target_pairs={{0,8},{8,16},{16,24},{24,32},{32,40},{40,48},{48,56},{56,64},{64,7... | collective-permute-start | bytes 1572872 | tf_op jit(solution)/shard_map/ppermute | solution.py:23
  19.9 17.0 %collective-permute-start.1 = (f32[1024,1,128]{2,0,1:T(8,128)S(1)}, f32[1024,1,128]{2,0,1:T(8,128)S(1)}, u32[]{:S(2)}, u32[]{:S(2)}) collective-permute-start(f32[1024,1,128]{2,0,1:T(8,128)S(1)} %get-tuple-element.10), channel_id=1, source_target_pairs={{8,0},{16,8},{24,16},{32,24},{40,32},{48,40},{56,48},{64,56},{72,6... | collective-permute-start | bytes 1572872 | tf_op jit(solution)/shard_map/ppermute | solution.py:24
  36.9 9.3 %copy-start = (f32[1024,18,128]{2,0,1:T(8,128)}, f32[1024,18,128]{2,0,1:T(8,128)S(1)}, u32[]{:S(2)}) copy-start(f32[1024,18,128]{2,0,1:T(8,128)S(1)} %constant_dynamic-update-slice_fusion) | copy-start | bytes 28311556
  51.8 10.2 %collective-permute-start.2 = (f32[1024,18,1]{0,2,1:T(1,128)S(1)}, f32[1024,18,1]{0,2,1:T(1,128)S(1)}, u32[]{:S(2)}, u32[]{:S(2)}) collective-permute-start(f32[1024,18,1]{0,2,1:T(1,128)S(1)} %copy.13), channel_id=1, source_target_pairs={{1,0},{2,1},{3,2},{4,3},{5,4},{6,5},{7,6},{9,8},{10,9},{11,10},{12... | collective-permute-start | bytes 221192 | tf_op jit(solution)/shard_map/ppermute | solution.py:24
  59.3 7.8 %collective-permute-start.3 = (f32[1024,18,1]{0,2,1:T(1,128)S(1)}, f32[1024,18,1]{0,2,1:T(1,128)S(1)}, u32[]{:S(2)}, u32[]{:S(2)}) collective-permute-start(f32[1024,18,1]{0,2,1:T(1,128)S(1)} %copy.15), channel_id=1, source_target_pairs={{0,1},{1,2},{2,3},{3,4},{4,5},{5,6},{6,7},{8,9},{9,10},{10,11},{11... | collective-permute-start | bytes 221192 | tf_op jit(solution)/shard_map/ppermute | solution.py:23
Sparse Core Ops, SparseCore 0:
  98.8 269.7 all-reduce.2
where the time goes:
time: 382 us; the launch traced here: 381 us
  waiting for transfers between devices  199 us (52%)
  blocking collectives  80.3 us (21%)
  local copies, waits for them, and re-layouts  46.3 us (12%)
  other arithmetic  22 us (6%)
  between operations  14.2 us (4%)
  matrix products  10.1 us (3%)
  starting transfers between devices  9.66 us (3%)
    psum x1, waiting for transfers between devices, on_device(): lax.psum(lax.dot_general(flat_patterns, stacked, (((1,), (1,)), ((), ()))...  189 us
    psum x1, blocking collectives, on_device(): energy = lax.psum(local_energy, ('lon', 'lat'))  80.3 us
    reduce_sum x1, other arithmetic, on_device(): local_energy = jnp.sum(east_vel * east_vel + north_vel * north_vel)  18.3 us
    unnamed x9, local copies, waits for them, and re-layouts  16.1 us
    slice x3, local copies, waits for them, and re-layouts, padded_2(): initial = lax.slice_in_dim(shard, 0, width, axis=dim)  14.1 us
    ppermute x2, waiting for transfers between devices, padded_2(): before = lax.ppermute(last, axis, up)  9.8 us
    dot_general x1, matrix products, on_device(): lax.dot_general(flat_patterns, stacked, (((1,), (1,)), ((), ())), preferr...  8.1 us
  transfers between devices with their start and end apart: 5, of which 2 were waited for; matrix products, arithmetic and copies ran while one was open for 4% of the time, Pallas kernels for 0%

commit v1 on v0

--- a/solution.py
+++ b/solution.py
@@ -1,3 +1,4 @@
+import functools
 import math
 import jax
 import jax.numpy as jnp
@@ -11,6 +12,15 @@
 LAT_SOUTH = 20.0
 LAT_SPAN = 45.0
 LON_STEP = 1.0 / 12.0
+
+
+def numbers_apply(own_rows, axis_key, bus_axis):
+    for w in (axis_key, bus_axis):
+        own_rows = lax.psum(own_rows, w)
+    return own_rows
+
+
+pack_the_seats_all = functools.partial(numbers_apply, axis_key="lon", bus_axis="lat")
 
 
 def padded_2(shard, sides, width):
@@ -63,11 +73,10 @@
     owned = mode_count // lat_devices
     flat_patterns = patterns.reshape(mode_count, 2 * lon_cells * lat_cells)
     energy = lax.psum(local_energy, ("lon", "lat"))
-    totals = lax.psum(
+    totals = pack_the_seats_all(
         lax.dot_general(
             flat_patterns, stacked, (((1,), (1,)), ((), ())), preferred_element_type=jnp.float32
-        ),
-        ("lon", "lat"),
+        )
     )
     cell_total = 2.0 * days * lon_cells * lon_devices * total_rows
     centered = totals - jnp.mean(totals, axis=1, keepdims=True)

time: 382 us -> 348 us (0.911)
  waiting for transfers between devices: 199 us -> 169 us
  blocking collectives: 80.3 us -> 72.8 us
    psum x1 -> x2, waiting for transfers between devices: 189 us -> 160 us  [numbers_apply(): own_rows = lax.psum(own_rows, w)]
    psum x1, blocking collectives: 80.3 us -> 72.8 us  [on_device(): energy = lax.psum(local_energy, ('lon', 'lat'))]
  transfers between devices with their start and end apart: 5 -> 6, of which waited for: 2 -> 2; matrix products, arithmetic and copies ran while one was open for 4% -> 5% of each run, Pallas kernels for 0% -> 0%
where the time goes in v1:
time: 348 us; the launch traced here: 345 us
  waiting for transfers between devices  169 us (49%)
  blocking collectives  72.8 us (21%)
  local copies, waits for them, and re-layouts  46.3 us (13%)
  other arithmetic  22 us (6%)
  between operations  14.2 us (4%)
  matrix products  10.1 us (3%)
  starting transfers between devices  9.7 us (3%)
    psum x2, waiting for transfers between devices, numbers_apply(): own_rows = lax.psum(own_rows, w)  160 us
    psum x1, blocking collectives, on_device(): energy = lax.psum(local_energy, ('lon', 'lat'))  72.8 us
    reduce_sum x1, other arithmetic, on_device(): local_energy = jnp.sum(east_vel * east_vel + north_vel * north_vel)  18.3 us
    unnamed x9, local copies, waits for them, and re-layouts  16.1 us
    slice x3, local copies, waits for them, and re-layouts, padded_2(): initial = lax.slice_in_dim(shard, 0, width, axis=dim)  14.1 us
    ppermute x2, waiting for transfers between devices, padded_2(): before = lax.ppermute(last, axis, up)  9.8 us
    dot_general x1, matrix products, on_device(): lax.dot_general(flat_patterns, stacked, (((1,), (1,)), ((), ())), preferr...  8.1 us
  transfers between devices with their start and end apart: 6, of which 2 were waited for; matrix products, arithmetic and copies ran while one was open for 5% of the time, Pallas kernels for 0%

profile of v1, /device:TPU:2, one launch (start us, length us, event | category | flops | bytes accessed | tf_op | source)
XLA Modules:
  0.0 344.6 jit_solution(16123550296219267547)
XLA Ops:
  6.5 0.0 copy-start.2
  6.5 0.0 all-reduce.4.cloned.1.call-start
  6.5 6.1 %copy.10 = f32[1024,16,128]{2,0,1:T(8,128)S(1)} copy(f32[1024,16,128]{2,1,0:T(8,128)} %param.3) | data formatting | bytes 16777216 | tf_op args[0]
  12.6 0.0 copy-start.1
  12.6 3.3 copy-done.1
  15.9 0.1 fusion.23
  16.0 3.9 %collective-permute-start = (f32[1024,1,128]{2,0,1:T(8,128)S(1)}, f32[1024,1,128]{2,0,1:T(8,128)S(1)}, u32[]{:S(2)}, u32[]{:S(2)}) collective-permute-start(f32[1024,1,128]{2,0,1:T(8,128)S(1)} %get-tuple-element.11), channel_id=1, source_target_pairs={{0,8},{8,16},{16,24},{24,32},{32,40},{40,48},{48,56},{56,64},{64,7... | collective-permute-start | bytes 1572872 | tf_op jit(solution)/shard_map/ppermute | solution.py:33
  19.9 1.3 collective-permute-start.1
  21.2 0.0 copy-done.2
  21.2 9.8 %collective-permute-done = f32[1024,1,128]{2,0,1:T(8,128)S(1)} collective-permute-done((f32[1024,1,128]{2,0,1:T(8,128)S(1)}, f32[1024,1,128]{2,0,1:T(8,128)S(1)}, u32[]{:S(2)}, u32[]{:S(2)}) %collective-permute-start) | collective-permute-done | bytes 524320 | tf_op jit(solution)/shard_map/ppermute | solution.py:33
  31.0 5.8 %constant_dynamic-update-slice_fusion.1 = f32[1024,18,128]{2,0,1:T(8,128)S(1)} fusion(f32[1024,18,128]{2,0,1:T(8,128)S(1)} %constant_dynamic-update-slice_fusion.2, f32[1024,16,128]{2,1,0:T(8,128)} %param.3), kind=kLoop, calls=%fused_computation.24 | loop fusion | bytes 16777216
  36.8 0.0 collective-permute-done.1
  36.9 0.0 copy-start
  36.9 8.4 %fusion.22 = (f32[1024,18,1]{2,0,1:T(8,128)}, f32[1024,18,1]{2,0,1:T(8,128)}) fusion(f32[1024,18,128]{2,0,1:T(8,128)S(1)} %constant_dynamic-update-slice_fusion), kind=kLoop, calls=%fused_computation.35 | loop fusion | bytes 294912 | tf_op jit(solution)/shard_map/slice | solution.py:32
  45.3 0.9 copy-done
  46.2 5.6 %copy.13 = f32[1024,18,1]{0,2,1:T(1,128)S(1)} copy(f32[1024,18,1]{2,0,1:T(8,128)} %get-tuple-element.8) | data formatting | bytes 147456 | tf_op jit(solution)/shard_map/slice | solution.py:32
  51.8 1.9 collective-permute-start.2
  53.7 5.6 %copy.15 = f32[1024,18,1]{0,2,1:T(1,128)S(1)} copy(f32[1024,18,1]{2,0,1:T(8,128)} %get-tuple-element.9) | data formatting | bytes 147456 | tf_op jit(solution)/shard_map/slice | solution.py:31
  59.3 2.6 collective-permute-start.3
  61.9 0.1 multiply_divide_fusion
  62.0 0.0 collective-permute-done.2
  62.0 5.1 %copy.14 = f32[1024,18,1]{2,0,1:T(8,128)} copy(f32[1024,18,1]{0,2,1:T(1,128)S(1)} %collective-permute-done.2) | data formatting | bytes 147456 | tf_op jit(solution)/shard_map/ppermute | solution.py:34
  67.1 0.0 collective-permute-done.3
  67.1 5.2 %copy.16 = f32[1024,18,1]{2,0,1:T(8,128)} copy(f32[1024,18,1]{0,2,1:T(1,128)S(1)} %collective-permute-done.3) | data formatting | bytes 147456 | tf_op jit(solution)/shard_map/ppermute | solution.py:33
  72.2 18.3 %add_reduce_fusion = (f32[]{:T(128)}, bf16[1024,16,128]{2,0,1:T(8,128)(2,1)S(1)}, bf16[1024,1,16,128]{3,0,2,1:T(8,128)(2,1)S(1)}) fusion(f32[16,128]{1,0:T(8,128)S(1)} %convert_element_type.18, f32[1024,16,128]{2,0,1:T(8,128)} %copy-done.1, f32[1024,1,128]{2,0,1:T(8,128)S(1)} %collective-permute-done, f32[1024,1,128]{2,0,1:T(8,128)S(1)} %collective-permute-done.1, ...), kind=kLoop, calls=%fused_computation.14 | loop fusion | flops 33554432 | bytes 27419652 | tf_op jit(solution)/shard_map/reduce_sum | solution.py:66
  90.5 8.1 %fusion.11 = f32[512,1024]{0,1:T(8,128)} fusion(bf16[512,2,16,128]{3,2,1,0:T(8,128)(2,1)} %param.5, bf16[1024,1,16,128]{3,0,2,1:T(8,128)(2,1)S(1)} %get-tuple-element.7, bf16[1024,1,16,128]{3,0,2,1:T(8,128)(2,1)S(1)} %bitcast.14), kind=kOutput, calls=%fused_computation.19 | convolution fusion | flops 4299161600 | bytes 14680064 | tf_op jit(solution)/shard_map/dot_general | solution.py:77
  98.6 0.0 all-reduce.4.cloned.1.call-update
  98.7 0.0 all-reduce.6.cloned.1.call-start
  98.7 159.6 %all-reduce.4.cloned.1.call-done = f32[512,1024]{0,1:T(8,128)} async-done(((f32[512,1024]{0,1:T(8,128)}), f32[512,1024]{0,1:T(8,128)}) %all-reduce.4.cloned.1.call-update) | async-done | bytes 2097168 | tf_op jit(solution)/shard_map/psum | solution.py:19
  258.3 0.0 all-reduce.6.cloned.1.call-update
  258.3 72.8 %psum.23 = f32[]{:T(128)} all-reduce(f32[]{:T(128)} %get-tuple-element.5), channel_id=1, replica_groups=mesh['lon'=32,'lat'=8] {'lon','lat'}, use_global_device_ids=true, to_apply=%region_4.0 | all-reduce | flops 1 | bytes 8 | tf_op jit(solution)/shard_map/psum | solution.py:75
  331.8 0.0 all-reduce.6.cloned.1.call-done
  331.8 1.8 reduce_sum.18
  333.6 1.9 subtract_divide_fusion
  335.5 0.2 constant_dynamic-slice_fusion
  335.7 2.0 fusion.16
  (4 shorter events, 0.1 us)
Async XLA Ops:
  6.5 14.6 %copy-start.2 = (s32[16,128]{1,0:T(8,128)S(1)}, s32[16,128]{1,0:T(8,128)}, u32[]{:S(2)}) copy-start(s32[16,128]{1,0:T(8,128)} %param.4) | copy-start | bytes 24580
  6.5 251.8 %all-reduce.4.cloned.1.call-start = ((), (), s32[]{:S(2)}) async-start(), calls=%async_computation | async-start | bytes 4194304 | tf_op jit(solution)/shard_map/psum | solution.py:19
  12.6 3.3 copy-start.1
  16.0 15.0 %collective-permute-start = (f32[1024,1,128]{2,0,1:T(8,128)S(1)}, f32[1024,1,128]{2,0,1:T(8,128)S(1)}, u32[]{:S(2)}, u32[]{:S(2)}) collective-permute-start(f32[1024,1,128]{2,0,1:T(8,128)S(1)} %get-tuple-element.11), channel_id=1, source_target_pairs={{0,8},{8,16},{16,24},{24,32},{32,40},{40,48},{48,56},{56,64},{64,7... | collective-permute-start | bytes 1572872 | tf_op jit(solution)/shard_map/ppermute | solution.py:33
  19.9 17.0 %collective-permute-start.1 = (f32[1024,1,128]{2,0,1:T(8,128)S(1)}, f32[1024,1,128]{2,0,1:T(8,128)S(1)}, u32[]{:S(2)}, u32[]{:S(2)}) collective-permute-start(f32[1024,1,128]{2,0,1:T(8,128)S(1)} %get-tuple-element.10), channel_id=1, source_target_pairs={{8,0},{16,8},{24,16},{32,24},{40,32},{48,40},{56,48},{64,56},{72,6... | collective-permute-start | bytes 1572872 | tf_op jit(solution)/shard_map/ppermute | solution.py:34
  36.9 9.3 %copy-start = (f32[1024,18,128]{2,0,1:T(8,128)}, f32[1024,18,128]{2,0,1:T(8,128)S(1)}, u32[]{:S(2)}) copy-start(f32[1024,18,128]{2,0,1:T(8,128)S(1)} %constant_dynamic-update-slice_fusion) | copy-start | bytes 28311556
  51.8 10.2 %collective-permute-start.2 = (f32[1024,18,1]{0,2,1:T(1,128)S(1)}, f32[1024,18,1]{0,2,1:T(1,128)S(1)}, u32[]{:S(2)}, u32[]{:S(2)}) collective-permute-start(f32[1024,18,1]{0,2,1:T(1,128)S(1)} %copy.13), channel_id=1, source_target_pairs={{1,0},{2,1},{3,2},{4,3},{5,4},{6,5},{7,6},{9,8},{10,9},{11,10},{12... | collective-permute-start | bytes 221192 | tf_op jit(solution)/shard_map/ppermute | solution.py:34
  59.3 7.8 %collective-permute-start.3 = (f32[1024,18,1]{0,2,1:T(1,128)S(1)}, f32[1024,18,1]{0,2,1:T(1,128)S(1)}, u32[]{:S(2)}, u32[]{:S(2)}) collective-permute-start(f32[1024,18,1]{0,2,1:T(1,128)S(1)} %copy.15), channel_id=1, source_target_pairs={{0,1},{1,2},{2,3},{3,4},{4,5},{5,6},{6,7},{8,9},{9,10},{10,11},{11... | collective-permute-start | bytes 221192 | tf_op jit(solution)/shard_map/ppermute | solution.py:33
  98.7 233.1 %all-reduce.6.cloned.1.call-start = ((), (), s32[]{:S(2)}) async-start(), calls=%async_computation.1 | async-start | bytes 4194304 | tf_op jit(solution)/shard_map/psum | solution.py:19
Sparse Core Ops, SparseCore 0:
  98.8 159.4 all-reduce.3
  260.7 65.8 all-reduce.5
